TPU v7x, 32 devices: a whole 2x2x4 slice. The times are simulated.
32 devices in a mesh: groups: 2 (over x), section: 2 (over core), tensor: 8 (over z, y).
Axes of the slice: x: 2, y: 2, z: 4, core: 2. Of those that a mesh axis runs over, the one named last changes fastest.
Arguments:
- hidden: bfloat16 [2, 1024, 26624], P('section', 'groups', 'tensor'), parts along dimension 1, may hold values from -6 to 6
- down_weight: bfloat16 [2, 26624, 8192], P('section', 'tensor'), may hold values from -0.0546875 to 0.0546875
- residual: bfloat16 [2, 1024, 8192], P('section', 'groups', 'tensor'), parts along dimension 1, may hold values from -100 to 100
- norm_gain: float32 [2, 8192], P('section'), may hold values from 0.1 to 1.9
- qkv_weight: bfloat16 [2, 8192, 9216], P('section', None, 'tensor'), may hold values from -0.0625 to 0.0625
Outputs:
- received: bfloat16 [2, 1024, 8192], P('section', 'groups', 'tensor'), parts along dimension 1
- projected: bfloat16 [2, 1024, 9216], P('section', 'groups', 'tensor'), parts along dimension 1
There are 2 independent parts, one for each index of `groups`. A program takes and returns all parts, laid end to end along the dimension named above; an argument that names none is the same for every part. Nothing has to cross between parts.
All inputs are finite; a program needn't handle non-finite values.
Results may differ from a plain program's by a relative error of at most 0.0057.
Values may be sent and summed in bfloat16 or wider, within the bound.
No kernel may reach another device: no remote copies, remote signals or barrier semaphores. Data moves between devices by JAX's collectives and lax.ppermute only.
A program may use at most 192 MiB of HBM per device.

v0:
```python
import jax
import jax.numpy as jnp
from jax import lax
from jax.sharding import PartitionSpec as P

D = 8192
epsilon = 1e-05


def shifted(value, axis, steps):
    count = lax.axis_size(axis)
    pairs = [(source, (source + steps) % count) for source in range(count)]
    return lax.ppermute(value, axis, pairs)


def normalize(floats, gain_part):
    square_sum = jnp.sum(floats * floats, axis=1, keepdims=True)
    scale_inv = lax.rsqrt(square_sum / D + epsilon)
    return (floats * scale_inv * gain_part[None, :]).astype(jnp.bfloat16)


def body(hidden, down_weight, residual, norm_gain, qkv_weight):
    hidden_local = hidden[0]
    down_local = down_weight[0]
    residual_local = residual[0]
    gain_full = norm_gain[0]
    qkv_local = qkv_weight[0]
    partial_sum = jnp.dot(hidden_local, down_local, preferred_element_type=jnp.float32)
    summed = lax.psum_scatter(partial_sum, "tensor", scatter_dimension=1, tiled=True)
    stream = (residual_local.astype(jnp.float32) + summed).astype(jnp.bfloat16)
    received = shifted(stream, "section", 1)
    gathered = lax.all_gather(received, "tensor", axis=1, tiled=True)
    normed = normalize(gathered.astype(jnp.float32), gain_full)
    projected = jnp.dot(normed, qkv_local, preferred_element_type=jnp.float32).astype(jnp.bfloat16)
    return (received[None], projected[None])


def solution(mesh):
    placed = (
        P("section", "groups", "tensor"),
        P("section", "tensor", None),
        P("section", "groups", "tensor"),
        P("section", None),
        P("section", None, "tensor"),
    )
    return jax.shard_map(
        body,
        mesh=mesh,
        in_specs=placed,
        out_specs=(P("section", "groups", "tensor"), P("section", "groups", "tensor")),
        check_vma=False,
    )
```

profile of v0, /device:TPU:0, one launch (start us, length us, event | category | flops | bytes accessed | tf_op | source)
XLA Modules:
  0.0 487.6 jit_solution(3447809766854134224)
XLA Ops:
  7.2 0.0 copy-start
  7.2 0.0 reduce-scatter.2.cloned.1.call-start
  7.2 1.9 copy-done
  9.1 35.6 %fusion = f32[512,8192]{1,0:T(8,128)} fusion(bf16[1,3328,8192]{2,1,0:T(8,128)(2,1)} %param.6, bf16[1,512,3328]{2,1,0:T(8,128)(2,1)S(1)} %copy-done), kind=kOutput, calls=%fused_computation | convolution fusion | flops 27917287424 | bytes 74711040 | tf_op jit(solution)/shard_map/dot_general | solution.py:28
  44.7 0.0 copy-start.4
  44.7 0.0 copy-start.5
  44.7 0.0 reduce-scatter.2.cloned.1.call-update
  44.7 0.0 all-gather.2.cloned.1.call-start
  44.8 283.0 %reduce-scatter.2.cloned.1.call-done = f32[512,1024]{1,0:T(8,128)} async-done(((f32[512,8192]{1,0:T(8,128)}), f32[512,1024]{1,0:T(8,128)}) %reduce-scatter.2.cloned.1.call-update) | async-done | bytes 2097168 | tf_op jit(solution)/shard_map/reduce_scatter | solution.py:29
  327.8 0.0 copy-done.4
  327.8 1.9 fusion.21
  329.8 0.1 collective-permute-start
  329.8 2.6 collective-permute-done
  332.5 0.0 copy-start.2
  332.5 1.0 copy-done.2
  333.5 0.0 all-gather.2.cloned.1.call-update
  333.5 123.7 %all-gather.2.cloned.1.call-done = bf16[512,8192]{1,0:T(8,128)(2,1)} async-done(((bf16[512,1024]{1,0:T(8,128)(2,1)}), bf16[512,8192]{1,0:T(8,128)(2,1)}) %all-gather.2.cloned.1.call-update) | async-done | bytes 8388624 | tf_op jit(solution)/shard_map/all_gather | solution.py:32
  457.2 5.1 %fusion.4 = f32[512]{0:T(512)S(1)} fusion(bf16[512,8192]{1,0:T(8,128)(2,1)} %all-gather.2.cloned.1.call-done), kind=kLoop, calls=%fused_computation.6 | loop fusion | flops 12582400 | bytes 8390656 | tf_op jit(solution)/shard_map/reduce_sum | solution.py:17
  462.3 0.0 copy-done.5
  462.3 0.0 copy-start.3
  462.3 0.0 copy-start.1
  462.3 17.5 %fusion.16 = bf16[1,512,1152]{2,1,0:T(8,128)(2,1)} fusion(bf16[1,8192,1152]{2,1,0:T(8,128)(2,1)} %param.9, bf16[512,8192]{1,0:T(8,128)(2,1)} %all-gather.2.cloned.1.call-done, f32[8192]{0:T(1024)S(1)} %bitcast.21, f32[512]{0:T(512)S(1)} %add_rsqrt_fusion), kind=kOutput, calls=%fused_computation.13 | convolution fusion | flops 9681043456 | bytes 28477440 | tf_op jit(solution)/shard_map/dot_general | solution.py:34
  479.8 0.0 copy-done.3
  479.8 1.0 copy.8
  480.8 0.0 copy-done.1
  (1 shorter events, 0.0 us)
Async XLA Ops:
  7.2 2.0 copy-start
  7.2 320.6 %reduce-scatter.2.cloned.1.call-start = ((), (), s32[]{:S(2)}) async-start(), calls=%async_computation.1 | async-start | bytes 18874368 | tf_op jit(solution)/shard_map/reduce_scatter | solution.py:29
  44.7 283.1 %copy-start.4 = (bf16[1,512,1024]{2,1,0:T(8,128)(2,1)S(1)}, bf16[1,512,1024]{2,1,0:T(8,128)(2,1)}, u32[]{:S(2)}) copy-start(bf16[1,512,1024]{2,1,0:T(8,128)(2,1)} %param.7) | copy-start | bytes 3145732
  44.7 417.6 %copy-start.5 = (f32[1,8192]{1,0:T(1,128)S(1)}, f32[1,8192]{1,0:T(1,128)}, u32[]{:S(2)}) copy-start(f32[1,8192]{1,0:T(1,128)} %param.8) | copy-start | bytes 98308
  44.7 412.4 %all-gather.2.cloned.1.call-start = ((), (), s32[]{:S(2)}) async-start(), calls=%async_computation.2 | async-start | bytes 9437184 | tf_op jit(solution)/shard_map/all_gather | solution.py:32
  329.8 2.7 collective-permute-start
  332.5 1.0 copy-start.2
  462.3 17.5 %copy-start.3 = (bf16[512,1024]{1,0:T(8,128)(2,1)S(1)}, bf16[512,1024]{1,0:T(8,128)(2,1)}, u32[]{:S(2)}) copy-start(bf16[512,1024]{1,0:T(8,128)(2,1)} %copy-done.2) | copy-start | bytes 3145732
  462.3 18.5 %copy-start.1 = (bf16[1,512,3328]{2,1,0:T(8,128)(2,1)S(1)}, bf16[1,512,3328]{2,1,0:T(8,128)(2,1)}, u32[]{:S(2)}) copy-start(bf16[1,512,3328]{2,1,0:T(8,128)(2,1)} %param.5) | copy-start | bytes 10223620
Sparse Core Ops, SparseCore 0:
  44.9 282.9 reduce-scatter.1
  333.6 123.5 all-gather.1
where the time goes:
time: 488 us
  waiting for transfers between devices  409 us (84%)
  matrix products  53 us (11%)
  between operations  14.1 us (3%)
  other arithmetic  7.05 us (1%)
    reduce_scatter x1, waiting for transfers between devices, body(): lax.psum_scatter(partial_sum, 'tensor', scatter_dimension=1, tiled=True)  283 us
    all_gather x1, waiting for transfers between devices, body(): gathered = lax.all_gather(received, 'tensor', axis=1, tiled=True)  124 us
    dot_general x1, matrix products, body(): jnp.dot(hidden_local, down_local, preferred_element_type=jnp.float32)  35.6 us
    dot_general x1, matrix products, body(): jnp.dot(normed, qkv_local, preferred_element_type=jnp.float32)  17.5 us
  transfers between devices with their start and end apart: 3, of which 3 were waited for; matrix products, arithmetic and copies ran while one was open for 0% of the time, Pallas kernels for 0%

commit v1 on v0

--- a/solution.py
+++ b/solution.py
@@ -5,6 +5,27 @@
 
 D = 8192
 epsilon = 1e-05
+
+
+def gather_around(x, axis, dim):
+    peers, index, span = (lax.axis_size(axis), lax.axis_index(axis), x.shape[dim])
+    ahead = [(i, (i + 1) % peers) for i in range(peers)]
+    backward = [(i, (i - 1) % peers) for i in range(peers)]
+    out = jnp.zeros((*x.shape[:dim], peers * span, *x.shape[dim + 1 :]), x.dtype)
+    out = lax.dynamic_update_slice_in_dim(out, x, index * span, axis=dim)
+    from_left = from_right = x
+    middle = peers // 2
+    for lap in range(1, middle + 1):
+        from_left = lax.ppermute(from_left, axis, ahead)
+        out = lax.dynamic_update_slice_in_dim(
+            out, from_left, (index - lap) % peers * span, axis=dim
+        )
+        if lap < peers - middle:
+            from_right = lax.ppermute(from_right, axis, backward)
+            out = lax.dynamic_update_slice_in_dim(
+                out, from_right, (index + lap) % peers * span, axis=dim
+            )
+    return out
 
 
 def shifted(value, axis, steps):
@@ -29,7 +50,7 @@
     summed = lax.psum_scatter(partial_sum, "tensor", scatter_dimension=1, tiled=True)
     stream = (residual_local.astype(jnp.float32) + summed).astype(jnp.bfloat16)
     received = shifted(stream, "section", 1)
-    gathered = lax.all_gather(received, "tensor", axis=1, tiled=True)
+    gathered = gather_around(received, "tensor", 1)
     normed = normalize(gathered.astype(jnp.float32), gain_full)
     projected = jnp.dot(normed, qkv_local, preferred_element_type=jnp.float32).astype(jnp.bfloat16)
     return (received[None], projected[None])

time: 488 us -> 526 us (1.078)
  waiting for transfers between devices: 409 us -> 430 us
  starting transfers between devices: 0.15 us -> 16.9 us
  local copies, waits for them, and re-layouts: 3.88 us -> 9.69 us
    ppermute x0 -> x7, waiting for transfers between devices: none -> 144 us  [the longest x4 144 us: gather_around(): from_left = lax.ppermute(from_left, axis, ahead)]
    all_gather x1 -> x0, waiting for transfers between devices: 124 us -> none  [body(): gathered = lax.all_gather(received, 'tensor', axis=1, tiled=True)]
    ppermute x0 -> x7, starting transfers between devices: none -> 16.8 us  [the longest x4 9 us: gather_around(): from_left = lax.ppermute(from_left, axis, ahead)]
    dynamic_update_slice x0 -> x8, local copies, waits for them, and re-layouts: none -> 5.77 us  [the longest x4 2.89 us: gather_around(): lax.dynamic_update_slice_in_dim(out, from_left, (index - lap) % peers * s...]
  transfers between devices with their start and end apart: 3 -> 9, of which waited for: 3 -> 6; matrix products, arithmetic and copies ran while one was open for 0% -> 1% of each run, Pallas kernels for 0% -> 0%
where the time goes in v1:
time: 526 us; the launch traced here: 525 us
  waiting for transfers between devices  430 us (82%)
  matrix products  51.1 us (10%)
  starting transfers between devices  16.9 us (3%)
  between operations  14.2 us (3%)
  local copies, waits for them, and re-layouts  9.69 us (2%)
    reduce_scatter x1, waiting for transfers between devices, body(): lax.psum_scatter(partial_sum, 'tensor', scatter_dimension=1, tiled=True)  283 us
    ppermute x4, waiting for transfers between devices, gather_around(): from_left = lax.ppermute(from_left, axis, ahead)  144 us
    dot_general x1, matrix products, body(): jnp.dot(hidden_local, down_local, preferred_element_type=jnp.float32)  35.6 us
    dot_general x1, matrix products, body(): jnp.dot(normed, qkv_local, preferred_element_type=jnp.float32)  15.5 us
  transfers between devices with their start and end apart: 9, of which 6 were waited for; matrix products, arithmetic and copies ran while one was open for 1% of the time, Pallas kernels for 0%

profile of v1, /device:TPU:0, one launch (start us, length us, event | category | flops | bytes accessed | tf_op | source)
XLA Modules:
  0.0 525.4 jit_solution(6086670701055181917)
XLA Ops:
  7.2 0.0 copy-start
  7.2 0.0 reduce-scatter.2.cloned.1.call-start
  7.2 1.9 copy-done
  9.1 35.6 %fusion = f32[512,8192]{1,0:T(8,128)} fusion(bf16[1,3328,8192]{2,1,0:T(8,128)(2,1)} %param.6, bf16[1,512,3328]{2,1,0:T(8,128)(2,1)S(1)} %copy-done), kind=kOutput, calls=%fused_computation | convolution fusion | flops 27917287424 | bytes 74711040 | tf_op jit(solution)/shard_map/dot_general | solution.py:49
  44.7 0.0 copy-start.6
  44.7 0.0 reduce-scatter.2.cloned.1.call-update
  44.7 283.1 %reduce-scatter.2.cloned.1.call-done = f32[512,1024]{1,0:T(8,128)} async-done(((f32[512,8192]{1,0:T(8,128)}), f32[512,1024]{1,0:T(8,128)}) %reduce-scatter.2.cloned.1.call-update) | async-done | bytes 2097168 | tf_op jit(solution)/shard_map/reduce_scatter | solution.py:50
  327.8 0.0 copy-done.6
  327.8 1.9 fusion.21
  329.8 0.1 collective-permute-start
  329.9 2.6 collective-permute-done
  332.5 0.0 copy-start.2
  332.5 1.5 collective-permute-start.1
  334.0 3.3 collective-permute-start.2
  337.2 41.9 %collective-permute-done.1 = bf16[512,1024]{1,0:T(8,128)(2,1)S(1)} collective-permute-done((bf16[512,1024]{1,0:T(8,128)(2,1)S(1)}, bf16[512,1024]{1,0:T(8,128)(2,1)S(1)}, u32[]{:S(2)}, u32[]{:S(2)}) %collective-permute-start.1) | collective-permute-done | bytes 1048608 | tf_op jit(solution)/shard_map/ppermute | solution.py:19
  379.2 2.5 collective-permute-start.3
  381.6 0.0 collective-permute-done.2
  381.6 2.2 collective-permute-start.4
  383.9 42.1 %collective-permute-done.3 = bf16[512,1024]{1,0:T(8,128)(2,1)S(1)} collective-permute-done((bf16[512,1024]{1,0:T(8,128)(2,1)S(1)}, bf16[512,1024]{1,0:T(8,128)(2,1)S(1)}, u32[]{:S(2)}, u32[]{:S(2)}) %collective-permute-start.3) | collective-permute-done | bytes 1048608 | tf_op jit(solution)/shard_map/ppermute | solution.py:19
  426.0 0.0 copy-start.4
  426.0 2.5 collective-permute-start.5
  428.5 0.0 collective-permute-done.4
  428.5 0.0 copy-done.4
  428.5 2.2 collective-permute-start.6
  430.7 41.9 %collective-permute-done.5 = bf16[512,1024]{1,0:T(8,128)(2,1)} collective-permute-done((bf16[512,1024]{1,0:T(8,128)(2,1)S(1)}, bf16[512,1024]{1,0:T(8,128)(2,1)}, u32[]{:S(2)}, u32[]{:S(2)}) %collective-permute-start.5) | collective-permute-done | bytes 1048608 | tf_op jit(solution)/shard_map/ppermute | solution.py:19
  472.6 2.6 collective-permute-start.7
  475.2 1.0 broadcast_in_dim.11
  476.2 0.1 constant_dynamic-update-slice_fusion.7
  476.3 0.1 constant_dynamic-update-slice_fusion.6
  476.4 0.1 constant_dynamic-update-slice_fusion.5
  476.6 0.0 copy-done.5
  476.6 0.1 constant_dynamic-update-slice_fusion.4
  476.7 0.0 copy-done.2
  476.7 0.0 copy-start.7
  476.7 1.3 constant_dynamic-update-slice_fusion.3
  478.1 1.3 constant_dynamic-update-slice_fusion.2
  479.4 0.0 collective-permute-done.6
  479.4 1.3 constant_dynamic-update-slice_fusion.1
  480.8 18.2 %collective-permute-done.7 = bf16[512,1024]{1,0:T(8,128)(2,1)} collective-permute-done((bf16[512,1024]{1,0:T(8,128)(2,1)}, bf16[512,1024]{1,0:T(8,128)(2,1)}, u32[]{:S(2)}, u32[]{:S(2)}) %collective-permute-start.7) | collective-permute-done | bytes 1048608 | tf_op jit(solution)/shard_map/ppermute | solution.py:19
  498.9 1.3 constant_dynamic-update-slice_fusion
  500.3 1.7 fusion.4
  502.0 0.0 copy-done.7
  502.0 0.0 copy-start.3
  502.0 0.0 copy-start.1
  502.0 15.5 %fusion.16 = bf16[1,512,1152]{2,1,0:T(8,128)(2,1)} fusion(bf16[1,8192,1152]{2,1,0:T(8,128)(2,1)} %param.9, bf16[512,8192]{1,0:T(8,128)(2,1)S(1)} %constant_dynamic-update-slice_fusion, f32[8192]{0:T(1024)S(1)} %bitcast.21, f32[512]{0:T(512)S(1)} %add_rsqrt_fusion), kind=kOutput, calls=%fused_computation.13 | convolution fusion | flops 9681043456 | bytes 28477440 | tf_op jit(solution)/shard_map/dot_general | solution.py:55
  517.5 0.0 copy-done.3
  517.5 1.0 copy.16
  518.5 0.0 copy-done.1
  (2 shorter events, 0.0 us)
Async XLA Ops:
  7.2 2.0 copy-start
  7.2 320.7 %reduce-scatter.2.cloned.1.call-start = ((), (), s32[]{:S(2)}) async-start(), calls=%async_computation.1 | async-start | bytes 18874368 | tf_op jit(solution)/shard_map/reduce_scatter | solution.py:50
  44.7 283.1 %copy-start.6 = (bf16[1,512,1024]{2,1,0:T(8,128)(2,1)S(1)}, bf16[1,512,1024]{2,1,0:T(8,128)(2,1)}, u32[]{:S(2)}) copy-start(bf16[1,512,1024]{2,1,0:T(8,128)(2,1)} %param.7) | copy-start | bytes 3145732
  329.8 2.7 collective-permute-start
  332.5 144.2 %copy-start.2 = (bf16[512,1024]{1,0:T(8,128)(2,1)}, bf16[512,1024]{1,0:T(8,128)(2,1)S(1)}, u32[]{:S(2)}) copy-start(bf16[512,1024]{1,0:T(8,128)(2,1)S(1)} %collective-permute-done) | copy-start | bytes 3145732
  332.5 46.6 %collective-permute-start.1 = (bf16[512,1024]{1,0:T(8,128)(2,1)S(1)}, bf16[512,1024]{1,0:T(8,128)(2,1)S(1)}, u32[]{:S(2)}, u32[]{:S(2)}) collective-permute-start(bf16[512,1024]{1,0:T(8,128)(2,1)S(1)} %collective-permute-done), channel_id=1, source_target_pairs={{0,1},{1,2},{2,3},{3,4},{4,5},{5,6},{6,7},{7,0},{8,9},{9,10},{10,1... | collective-permute-start | bytes 3145736 | tf_op jit(solution)/shard_map/ppermute | solution.py:19
  334.0 47.7 %collective-permute-start.2 = (bf16[512,1024]{1,0:T(8,128)(2,1)S(1)}, bf16[512,1024]{1,0:T(8,128)(2,1)S(1)}, u32[]{:S(2)}, u32[]{:S(2)}) collective-permute-start(bf16[512,1024]{1,0:T(8,128)(2,1)S(1)} %collective-permute-done), channel_id=1, source_target_pairs={{0,7},{1,0},{2,1},{3,2},{4,3},{5,4},{6,5},{7,6},{8,15},{9,8},{10,9... | collective-permute-start | bytes 3145736 | tf_op jit(solution)/shard_map/ppermute | solution.py:24
  379.2 46.8 %collective-permute-start.3 = (bf16[512,1024]{1,0:T(8,128)(2,1)S(1)}, bf16[512,1024]{1,0:T(8,128)(2,1)S(1)}, u32[]{:S(2)}, u32[]{:S(2)}) collective-permute-start(bf16[512,1024]{1,0:T(8,128)(2,1)S(1)} %collective-permute-done.1), channel_id=1, source_target_pairs={{0,1},{1,2},{2,3},{3,4},{4,5},{5,6},{6,7},{7,0},{8,9},{9,10},{10,1... | collective-permute-start | bytes 3145736 | tf_op jit(solution)/shard_map/ppermute | solution.py:19
  381.6 46.8 %collective-permute-start.4 = (bf16[512,1024]{1,0:T(8,128)(2,1)S(1)}, bf16[512,1024]{1,0:T(8,128)(2,1)}, u32[]{:S(2)}, u32[]{:S(2)}) collective-permute-start(bf16[512,1024]{1,0:T(8,128)(2,1)S(1)} %collective-permute-done.2), channel_id=1, source_target_pairs={{0,7},{1,0},{2,1},{3,2},{4,3},{5,4},{6,5},{7,6},{8,15},{9,8},{10,9... | collective-permute-start | bytes 3145736 | tf_op jit(solution)/shard_map/ppermute | solution.py:24
  426.0 2.5 copy-start.4
  426.0 46.6 %collective-permute-start.5 = (bf16[512,1024]{1,0:T(8,128)(2,1)S(1)}, bf16[512,1024]{1,0:T(8,128)(2,1)}, u32[]{:S(2)}, u32[]{:S(2)}) collective-permute-start(bf16[512,1024]{1,0:T(8,128)(2,1)S(1)} %collective-permute-done.3), channel_id=1, source_target_pairs={{0,1},{1,2},{2,3},{3,4},{4,5},{5,6},{6,7},{7,0},{8,9},{9,10},{10,1... | collective-permute-start | bytes 3145736 | tf_op jit(solution)/shard_map/ppermute | solution.py:19
  428.5 50.9 %collective-permute-start.6 = (bf16[512,1024]{1,0:T(8,128)(2,1)}, bf16[512,1024]{1,0:T(8,128)(2,1)}, u32[]{:S(2)}, u32[]{:S(2)}) collective-permute-start(bf16[512,1024]{1,0:T(8,128)(2,1)} %collective-permute-done.4), channel_id=1, source_target_pairs={{0,7},{1,0},{2,1},{3,2},{4,3},{5,4},{6,5},{7,6},{8,15},{9,8},{10,9... | collective-permute-start | bytes 3145736 | tf_op jit(solution)/shard_map/ppermute | solution.py:24
  472.6 26.3 %collective-permute-start.7 = (bf16[512,1024]{1,0:T(8,128)(2,1)}, bf16[512,1024]{1,0:T(8,128)(2,1)}, u32[]{:S(2)}, u32[]{:S(2)}) collective-permute-start(bf16[512,1024]{1,0:T(8,128)(2,1)} %collective-permute-done.5), channel_id=1, source_target_pairs={{0,1},{1,2},{2,3},{3,4},{4,5},{5,6},{6,7},{7,0},{8,9},{9,10},{10,1... | collective-permute-start | bytes 3145736 | tf_op jit(solution)/shard_map/ppermute | solution.py:19
  475.2 1.4 copy-start.5
  476.7 25.3 %copy-start.7 = (f32[1,8192]{1,0:T(1,128)S(1)}, f32[1,8192]{1,0:T(1,128)}, u32[]{:S(2)}) copy-start(f32[1,8192]{1,0:T(1,128)} %param.8) | copy-start | bytes 98308
  502.0 15.5 %copy-start.3 = (bf16[512,1024]{1,0:T(8,128)(2,1)S(1)}, bf16[512,1024]{1,0:T(8,128)(2,1)}, u32[]{:S(2)}) copy-start(bf16[512,1024]{1,0:T(8,128)(2,1)} %copy-done.2) | copy-start | bytes 3145732
  502.0 16.5 %copy-start.1 = (bf16[1,512,3328]{2,1,0:T(8,128)(2,1)S(1)}, bf16[1,512,3328]{2,1,0:T(8,128)(2,1)}, u32[]{:S(2)}) copy-start(bf16[1,512,3328]{2,1,0:T(8,128)(2,1)} %param.5) | copy-start | bytes 10223620
Sparse Core Ops, SparseCore 0:
  44.9 282.9 reduce-scatter.1
